TPU v7x, 32 devices: a whole 2x2x4 slice. The times are simulated.
32 devices in a mesh: dp: 4 (over z), tensor: 8 (over y, x, core).
Axes of the slice: x: 2, y: 2, z: 4, core: 2. Of those that a mesh axis runs over, the one named last changes fastest.
Arguments:
- frames: bfloat16 [4, 16, 1024, 512], P(None, 'dp'), may hold values from -6 to 6
- cotangent: bfloat16 [4, 16, 1024, 512], P(None, 'dp'), may hold values from -6 to 6
- lengths: int32 [4, 16], P(None, 'dp'), may hold values from 1 to 1024, 12288 in all within a row
- expand_weight: float32 [512, 1536], P('dp', 'tensor'), may hold values from -0.25 to 0.25
- expand_first: float32 [512, 1536], P('dp', 'tensor'), may hold values from -384 to 384
- expand_second: float32 [512, 1536], P('dp', 'tensor'), may hold values from 3932.16 to 29491.2
- project_weight: float32 [1536, 512], P('tensor', 'dp'), may hold values from -0.15625 to 0.15625
- project_first: float32 [1536, 512], P('tensor', 'dp'), may hold values from -640 to 640
- project_second: float32 [1536, 512], P('tensor', 'dp'), may hold values from 9830.4 to 58982.4
- hidden_bias: float32 [1536], P('tensor'), may hold values from -3 to 3
- hidden_bias_first: float32 [1536], P('tensor'), may hold values from -384 to 384
- hidden_bias_second: float32 [1536], P('tensor'), may hold values from 3932.16 to 29491.2
- channel_param: float32 [12, 512], P(None, 'dp'), may hold values from -2 to 2
- channel_first: float32 [12, 512], P(None, 'dp'), may hold values from -768 to 768
- channel_second: float32 [12, 512], P(None, 'dp'), may hold values from 9830.4 to 73728
Outputs:
- block_out: bfloat16 [4, 16, 1024, 512], P(None, 'dp')
- frames_grad: bfloat16 [4, 16, 1024, 512], P(None, 'dp')
- expand_new: float32 [512, 1536], P('dp', 'tensor')
- expand_first_new: float32 [512, 1536], P('dp', 'tensor')
- expand_second_new: float32 [512, 1536], P('dp', 'tensor')
- expand_low: bfloat16 [512, 1536], P('dp', 'tensor')
- project_new: float32 [1536, 512], P('tensor', 'dp')
- project_first_new: float32 [1536, 512], P('tensor', 'dp')
- project_second_new: float32 [1536, 512], P('tensor', 'dp')
- project_low: bfloat16 [1536, 512], P('tensor', 'dp')
- bias_new: float32 [1536], P('tensor')
- bias_first_new: float32 [1536], P('tensor')
- bias_second_new: float32 [1536], P('tensor')
- channel_new: float32 [12, 512], P(None, 'dp')
- channel_first_new: float32 [12, 512], P(None, 'dp')
- channel_second_new: float32 [12, 512], P(None, 'dp')
Inputs may be any that keep to these rules, and one draw needn't show every extreme that they name: `lengths`: in each micro-batch the 16 true frame counts sum to 12288 and the largest is 1024.
All inputs are finite; a program needn't handle non-finite values. No bound on the sum of `lengths` on one device may be relied on, other than what follows from the above.
Results may differ from a plain program's by a relative error of at most 0.015.
Values may be sent and summed in bfloat16 or wider, within the bound.
A program may use at most 512 MiB of HBM per device.

v0:
```python
import jax
import jax.numpy as jnp
from jax import lax
from jax.sharding import PartitionSpec as P

eps_norm = 1e-06
beta_first = 0.5
beta_second = 0.5
adam_eps = 1e-08
decay_rate = 0.01
step_count = 6


def gelu_exact(value):
    return jax.nn.gelu(value, approximate=False)


def adam_update(weight, first, second, grad, rate):
    first_new = beta_first * first + (1.0 - beta_first) * grad
    second_new = beta_second * second + (1.0 - beta_second) * grad * grad
    first_hat = first_new / (1.0 - beta_first**step_count)
    second_hat = second_new / (1.0 - beta_second**step_count)
    weight_new = weight - rate * (
        first_hat / (jnp.sqrt(second_hat) + adam_eps) + decay_rate * weight
    )
    return (weight_new, first_new, second_new)


def contract_rows(left, right):
    return lax.dot_general(
        left, right, (((0,), (0,)), ((), ())), preferred_element_type=jnp.float32
    )


def contract_cols(left, right):
    return lax.dot_general(
        left, right, (((1,), (1,)), ((), ())), preferred_element_type=jnp.float32
    )


def per_device(
    frames,
    cotangent,
    lengths,
    expand_weight,
    expand_first,
    expand_second,
    project_weight,
    project_first,
    project_second,
    hidden_bias,
    hidden_bias_first,
    hidden_bias_second,
    channel_param,
    channel_first,
    channel_second,
):
    channel_full = lax.all_gather(channel_param, "dp", axis=1, tiled=True)
    taps = channel_full[0:7]
    kernel_bias = channel_full[7]
    norm_gain = channel_full[8]
    norm_shift = channel_full[9]
    out_bias = channel_full[10]
    layer_scale = channel_full[11]
    expand_bf = expand_weight.astype(jnp.bfloat16)
    project_bf = project_weight.astype(jnp.bfloat16)
    micro, clips, length, width = frames.shape
    hidden_part = expand_weight.shape[1]
    positions = lax.broadcasted_iota(jnp.int32, (clips, length), 1)
    grad_expand = jnp.zeros((width, hidden_part), jnp.float32)
    grad_project = jnp.zeros((hidden_part, width), jnp.float32)
    grad_channel = jnp.zeros((12, width), jnp.float32)
    grad_bias = jnp.zeros((hidden_part,), jnp.float32)
    out_list = []
    back_list = []
    for index in range(micro):
        expand_full, project_full = (
            lax.all_gather(expand_bf, "dp", axis=0, tiled=True),
            lax.all_gather(project_bf, "dp", axis=1, tiled=True),
        )
        mask = (positions < lengths[index][:, None]).astype(jnp.float32)[:, :, None]
        inputs = frames[index].astype(jnp.float32)
        masked = inputs * mask
        padded = jnp.pad(masked, ((0, 0), (3, 3), (0, 0)))
        conv = kernel_bias + sum((taps[k] * padded[:, k : k + length] for k in range(7)))
        mean = jnp.mean(conv, axis=-1, keepdims=True)
        centered = conv - mean
        var = jnp.mean(centered * centered, axis=-1, keepdims=True)
        inv_std = lax.rsqrt(var + eps_norm)
        nhat = centered * inv_std
        normed = (nhat * norm_gain + norm_shift).astype(jnp.bfloat16).reshape(clips * length, width)
        back = cotangent[index].astype(jnp.float32) * mask
        back_flat = back.reshape(clips * length, width)
        dz = layer_scale * back_flat
        dz_bf = dz.astype(jnp.bfloat16)
        pre = jnp.dot(normed, expand_full, preferred_element_type=jnp.float32) + hidden_bias
        gelu_out, gelu_back = jax.vjp(gelu_exact, pre)
        hidden = gelu_out.astype(jnp.bfloat16)
        partial_out = jnp.dot(hidden, project_full, preferred_element_type=jnp.float32)
        branch = lax.psum(partial_out.astype(jnp.bfloat16), "tensor").astype(jnp.float32)
        total = branch + out_bias
        piece_project = contract_rows(hidden, dz_bf)
        dhidden = contract_cols(dz_bf, project_full)
        dpre = gelu_back(dhidden)[0]
        piece_bias = jnp.sum(dpre, axis=0)
        dpre_bf = dpre.astype(jnp.bfloat16)
        piece_expand = contract_rows(normed, dpre_bf)
        dnormed_part = contract_cols(dpre_bf, expand_full)
        dnormed_flat = lax.psum(dnormed_part.astype(jnp.bfloat16), "tensor").astype(jnp.float32)
        outputs = (inputs + layer_scale * total.reshape(clips, length, width)) * mask
        out_list.append(outputs.astype(jnp.bfloat16))
        grad_scale = jnp.sum(back_flat * total, axis=0)
        grad_outb = jnp.sum(dz, axis=0)
        grad_bias = grad_bias + piece_bias
        dnormed = dnormed_flat.reshape(clips, length, width)
        grad_gain = jnp.sum(dnormed * nhat, axis=(0, 1))
        grad_shift = jnp.sum(dnormed, axis=(0, 1))
        dscaled = dnormed * norm_gain
        dconv = inv_std * (
            dscaled
            - jnp.mean(dscaled, axis=-1, keepdims=True)
            - nhat * jnp.mean(dscaled * nhat, axis=-1, keepdims=True)
        )
        grad_kbias = jnp.sum(dconv, axis=(0, 1))
        grad_taps = jnp.stack(
            [jnp.sum(dconv * padded[:, k : k + length], axis=(0, 1)) for k in range(7)], axis=0
        )
        dpadded = jnp.pad(dconv, ((0, 0), (3, 3), (0, 0)))
        dmasked = sum((taps[k] * dpadded[:, 6 - k : 6 - k + length] for k in range(7)))
        back_list.append((back + dmasked * mask).astype(jnp.bfloat16))
        piece_channel = jnp.concatenate(
            [
                grad_taps,
                grad_kbias[None],
                grad_gain[None],
                grad_shift[None],
                grad_outb[None],
                grad_scale[None],
            ],
            axis=0,
        )
        grad_expand = grad_expand + piece_expand
        grad_project = grad_project + piece_project
        grad_channel = grad_channel + piece_channel
    shard_expand, shard_project, shard_channel = (
        lax.psum_scatter(
            grad_expand.astype(jnp.bfloat16), "dp", scatter_dimension=0, tiled=True
        ).astype(jnp.float32),
        lax.psum_scatter(
            grad_project.astype(jnp.bfloat16), "dp", scatter_dimension=1, tiled=True
        ).astype(jnp.float32),
        lax.psum_scatter(
            grad_channel.astype(jnp.bfloat16), "dp", scatter_dimension=1, tiled=True
        ).astype(jnp.float32),
    )
    bias_total = lax.psum(grad_bias, "dp")
    e_new, e_first, e_second = adam_update(
        expand_weight, expand_first, expand_second, shard_expand, 0.02
    )
    p_new, p_first, p_second = adam_update(
        project_weight, project_first, project_second, shard_project, 0.01
    )
    b_new, b_first, b_second = adam_update(
        hidden_bias, hidden_bias_first, hidden_bias_second, bias_total, 0.1
    )
    c_new, c_first, c_second = adam_update(
        channel_param, channel_first, channel_second, shard_channel, 0.2
    )
    return (
        jnp.stack(out_list, axis=0),
        jnp.stack(back_list, axis=0),
        e_new,
        e_first,
        e_second,
        e_new.astype(jnp.bfloat16),
        p_new,
        p_first,
        p_second,
        p_new.astype(jnp.bfloat16),
        b_new,
        b_first,
        b_second,
        c_new,
        c_first,
        c_second,
    )


def solution(mesh):
    in_specs = (
        P(None, "dp", None, None),
        P(None, "dp", None, None),
        P(None, "dp"),
        P("dp", "tensor"),
        P("dp", "tensor"),
        P("dp", "tensor"),
        P("tensor", "dp"),
        P("tensor", "dp"),
        P("tensor", "dp"),
        P("tensor"),
        P("tensor"),
        P("tensor"),
        P(None, "dp"),
        P(None, "dp"),
        P(None, "dp"),
    )
    out_specs = (
        P(None, "dp", None, None),
        P(None, "dp", None, None),
        P("dp", "tensor"),
        P("dp", "tensor"),
        P("dp", "tensor"),
        P("dp", "tensor"),
        P("tensor", "dp"),
        P("tensor", "dp"),
        P("tensor", "dp"),
        P("tensor", "dp"),
        P("tensor"),
        P("tensor"),
        P("tensor"),
        P(None, "dp"),
        P(None, "dp"),
        P(None, "dp"),
    )
    return jax.shard_map(
        per_device, mesh=mesh, in_specs=in_specs, out_specs=out_specs, check_vma=False
    )
```

profile of v0, /device:TPU:0, one launch (start us, length us, event | category | flops | bytes accessed | tf_op | source)
XLA Modules:
  0.0 1032.3 jit_solution(2472263985125396175)
XLA Ops:
  8.9 15.0 %all_gather.6 = f32[12,512]{1,0:T(8,128)S(1)} all-gather(f32[12,128]{1,0:T(8,128)} %param.27), channel_id=1, replica_groups=mesh['dp'=4,'tensor'=8] {'dp'}, dimensions={1}, use_global_device_ids=true | all-gather | bytes 30720 | tf_op jit(solution)/shard_map/all_gather | solution.py:58
  28.4 13.4 %all_gather.8 = bf16[192,512]{1,0:T(8,128)(2,1)} all-gather(bf16[192,128]{1,0:T(8,128)(2,1)S(1)} %convert_element_type.318), channel_id=1, replica_groups=mesh['dp'=4,'tensor'=8] {'dp'}, dimensions={1}, use_global_device_ids=true | all-gather | bytes 245760 | tf_op jit(solution)/shard_map/all_gather | solution.py:79
  41.7 13.1 %all_gather.7 = bf16[512,192]{0,1:T(8,128)(2,1)} all-gather(bf16[128,192]{0,1:T(8,128)(2,1)S(1)} %convert_element_type.316), channel_id=1, replica_groups=mesh['dp'=4,'tensor'=8] {'dp'}, dimensions={0}, use_global_device_ids=true | all-gather | bytes 245760 | tf_op jit(solution)/shard_map/all_gather | solution.py:78
  54.9 16.1 %fusion.2 = (f32[4,1024,512]{2,1,0:T(8,128)}, f32[4,1024,512]{2,1,0:T(8,128)}, f32[4,1024,512]{2,1,0:T(8,128)}, f32[4,1024,512]{2,1,0:T(8,128)}) fusion(f32[4,1024]{1,0:T(4,128)S(1)} %get-tuple-element.190, bf16[4,4,1024,512]{3,2,1,0:T(8,128)(2,1)} %param.15, f32[4,1024]{1,0:T(4,128)S(1)} %get-tuple-element.199, f32[4,1024]{1,0:T(4,128)S(1)} %get-tuple-element.194, ...), kind=kLoop, calls=%fused_computation.12 | loop fusion | flops 16777216 | bytes 50397184 | tf_op jit(solution)/shard_map/mul | solution.py:83
  71.1 82.5 %fusion.97 = (f32[4,1024]{1,0:T(4,128)S(1)}, f32[4,1024,512]{2,1,0:T(8,128)S(1)}, f32[4,1024]{1,0:T(4,128)S(1)}, f32[4,1024,512]{2,1,0:T(8,128)S(1)}, f32[4,1024...) fusion(f32[512]{0:T(512)S(1)} %bitcast.296, f32[512]{0:T(512)S(1)} %bitcast.299, ...), kind=kLoop, calls=%fused_computation.319 | loop fusion | flops 125812736 | bytes 67190784 | tf_op jit(solution)/shard_map/reduce_sum | solution.py:86
  153.7 9.9 multiply_reduce_fusion.48
  163.7 1.6 copy-done.2
  165.3 1.3 multiply_reduce_fusion.49
  166.7 1.5 multiply_reduce_fusion.50
  168.2 1.5 multiply_reduce_fusion.51
  170.6 7.9 add_convert_fusion.3
  178.6 6.9 convolution_add_fusion.2
  185.5 3.2 convolution_add_fusion.3
  188.7 3.3 convolution_add_fusion.1
  192.1 3.2 convolution_add_fusion
  195.3 7.2 multiply_convert_fusion.3
  202.5 10.7 %fusion.91 = (f32[192]{0:T(256)}, bf16[4096,192]{0,1:T(8,128)(2,1)}, f32[4096,192]{0,1:T(8,128)S(1)}) fusion(f32[4096,192]{0,1:T(8,128)S(1)} %copy-done.29, bf16[4096,512]{1,0:T(8,128)(2,1)S(1)} %get-tuple-element.134, bf16[192,512]{1,0:T(8,128)(2,1)S(1)} %copy-done.38), kind=kOutput, calls=%fused_computation.316 | convolution fusion | flops 862715712 | bytes 12256000 | tf_op jit(solution)/shard_map/dot_general | solution.py:36
  213.7 1.4 copy-done.28
  215.1 9.6 fusion.89
  225.2 1.7 copy-done.18
  227.9 9.6 fusion.87
  238.9 1.5 copy-done.26
  240.4 9.8 fusion.85
  250.6 1.0 convolution_add_fusion.9
  251.7 1.0 convolution_add_fusion.8
  254.6 3.8 fusion.68
  264.9 3.3 convolution_convert_fusion.4
  268.2 3.3 convolution_convert_fusion
  271.5 3.2 convolution_convert_fusion.5
  274.7 3.3 convolution_convert_fusion.1
  278.0 3.2 convolution_convert_fusion.7
  281.3 3.3 convolution_convert_fusion.3
  284.6 3.2 convolution_convert_fusion.6
  287.9 3.2 convolution_convert_fusion.2
  291.8 9.4 psum.71
  305.3 388.8 %all-reduce.11.cloned.1.call-done = (bf16[4096,512]{1,0:T(8,128)(2,1)}, bf16[4096,512]{1,0:T(8,128)(2,1)}, bf16[4096,512]{1,0:T(8,128)(2,1)}, bf16[4096,512]{1,0...) async-done(((bf16[4096,512]{1,0:T(8,128)(2,1)}, bf16[4096,512]{1,0:T(8,128)(2,1)}, ...) | async-done | bytes 33554448 | tf_op jit(solution)/shard_map/psum | solution.py:100
  694.1 15.6 %multiply_reduce_fusion.12 = (f32[512]{0:T(512)S(1)}, f32[4,1024]{1,0:T(4,128)S(1)}, f32[4,1024]{1,0:T(4,128)S(1)}, f32[512]{0:T(512)S(1)}) fusion(f32[4,1024,512]{2,1,0:T(8,128)} %get-tuple-element.162, f32[4,1024]{1,0:T(4,128)S(1)} %copy-done.62, f32[4,1024]{1,0:T(4,128)S(1)} %copy-done.44, bf16[4096,512]{1,0:T(8,128)(2,1)} %get-tuple-element.83, ...), kind=kLoop, calls=%fused_computation.50 | loop fusion | flops 37739520 | bytes 33658880 | tf_op jit(solution)/shard_map/reduce_sum | solution.py:116
  709.8 4.8 convert_reduce_fusion
  714.8 40.5 %multiply_reduce_fusion.13 = (f32[512]{0:T(512)S(1)}, f32[512]{0:T(512)S(1)}, f32[512]{0:T(512)S(1)}, f32[512]{0:T(512)S(1)}, f32[512]{0:T(512)S(1)}, /*index=5*...) fusion(f32[4,1024,512]{2,1,0:T(8,128)} %get-tuple-element.137, ...), kind=kLoop, calls=%fused_computation.51 | loop fusion | flops 60809728 | bytes 46268416 | tf_op jit(solution)/shard_map/reduce_sum | solution.py:126
  755.4 42.4 %multiply_reduce_fusion.2 = (f32[512]{0:T(512)S(1)}, f32[4,1024]{1,0:T(4,128)S(1)}, f32[512]{0:T(512)S(1)}, f32[512]{0:T(512)S(1)}, f32[512]{0:T(512)S(1)}, /*in...) fusion(f32[4,1024,512]{2,1,0:T(8,128)} %get-tuple-element.164, ...), kind=kLoop, calls=%fused_computation.40 | loop fusion | flops 60809728 | bytes 46268416 | tf_op jit(solution)/shard_map/reduce_sum | solution.py:116
  797.9 28.1 %multiply_reduce_fusion.23 = (f32[512]{0:T(512)S(1)}, f32[512]{0:T(512)S(1)}, f32[512]{0:T(512)S(1)}, f32[512]{0:T(512)S(1)}, f32[512]{0:T(512)S(1)}, /*index=5*...) fusion(f32[4,1024,512]{2,1,0:T(8,128)} %get-tuple-element.136, f32[4,1024]{1,0:T(4,128)S(1)} %broadcast_multiply_fusion.6, ...), kind=kLoop, calls=%fused_computation.61 | loop fusion | flops 44036608 | bytes 29442048 | tf_op jit(solution)/shard_map/reduce_sum | solution.py:126
  826.1 67.0 %fusion.32 = (bf16[1,4,1024,512]{3,2,1,0:T(8,128)(2,1)}, bf16[1,4,1024,512]{3,2,1,0:T(8,128)(2,1)}, bf16[1,4,1024,512]{3,2,1,0:T(8,128)(2,1)}) fusion(f32[4,1024]{1,0:T(4,128)S(1)} %copy-done.48, f32[512]{0:T(512)S(1)} %bitcast.297, f32[512]{0:T(512)S(1)} %bitcast.300, f32[512]{0:T(512)S(1)} %bitcast.303, f32[4,1024,512]{2,1,0:T(8,128)} %get-tuple-element.181, ...), kind=kLoop, calls=%fused_computation.174 | loop fusion | flops 106954752 | bytes 50395136 | tf_op jit(solution)/shard_map/stack | solution.py:171
  893.1 48.9 %multiply_reduce_fusion.26 = (f32[512]{0:T(512)S(1)}, f32[512]{0:T(512)S(1)}, f32[512]{0:T(512)S(1)}, f32[512]{0:T(512)S(1)}, f32[512]{0:T(512)S(1)}, /*index=5*...) fusion(f32[4,1024,512]{2,1,0:T(8,128)} %get-tuple-element.89, ...), kind=kLoop, calls=%fused_computation.64 | loop fusion | flops 81782272 | bytes 71462912 | tf_op jit(solution)/shard_map/reduce_sum | solution.py:126
  942.1 10.2 fusion.35
  952.3 19.5 %multiply_reduce_fusion.20 = (f32[512]{0:T(512)S(1)}, f32[512]{0:T(512)S(1)}, f32[512]{0:T(512)S(1)}, f32[512]{0:T(512)S(1)}, f32[4096,512]{1,0:T(8,128)S(1)}, /...) fusion(f32[4096]{0:T(1024)S(1)} %bitcast.282, bf16[4,4,1024,512]{3,2,1,0:T(8,128)(2,1)} %param.16, ...), kind=kLoop, calls=%fused_computation.58 | loop fusion | flops 50329600 | bytes 67184640 | tf_op jit(solution)/shard_map/reduce_sum | solution.py:112
  971.7 26.7 %fusion.1 = (bf16[1,4,1024,512]{3,2,1,0:T(8,128)(2,1)}, bf16[1,4,1024,512]{3,2,1,0:T(8,128)(2,1)}, bf16[1,4,1024,512]{3,2,1,0:T(8,128)(2,1)}, bf16[1,4,1024,512]...) fusion(f32[4,1024]{1,0:T(4,128)S(1)} %copy-done.48, ...), kind=kLoop, calls=%fused_computation.11 | loop fusion | flops 75495424 | bytes 83961856 | tf_op jit(solution)/shard_map/convert_element_type | solution.py:111
  999.5 16.8 %pad_maximum_fusion.1 = bf16[4,4,1024,512]{3,2,1,0:T(8,128)(2,1)} fusion(bf16[1,4,1024,512]{3,2,1,0:T(8,128)(2,1)} %fusion.35, bf16[1,4,1024,512]{3,2,1,0:T(8,128)(2,1)} %get-tuple-element.126, bf16[1,4,1024,512]{3,2,1,0:T(8,128)(2,1)} %get-tuple-element.125, bf16[1,4,1024,512]{3,2,1,0:T(8,128)(2,1)} %get-tuple-element.124), kind=kLoop, calls=%fused_computation.1 | loop fusion | flops 25165824 | bytes 33554432 | tf_op jit(solution)/shard_map/stack | solution.py:171
  1016.4 7.0 pad_maximum_fusion
  (278 shorter events, 25.5 us)
Async XLA Ops:
  8.0 293.8 %reduce-scatter.12.cloned.1.call-start = ((), (), s32[]{:S(2)}) async-start(), calls=%async_computation.4 | async-start | bytes 327680
  24.5 46.6 %copy-start.79 = (f32[1,512]{1,0:T(1,128)}, f32[1,512]{1,0:T(1,128)S(1)}, u32[]{:S(2)}) copy-start(f32[1,512]{1,0:T(1,128)S(1)} %get-tuple-element.150) | copy-start | bytes 6148
  24.5 46.6 %copy-start.81 = (f32[1,512]{1,0:T(1,128)}, f32[1,512]{1,0:T(1,128)S(1)}, u32[]{:S(2)}) copy-start(f32[1,512]{1,0:T(1,128)S(1)} %get-tuple-element.151) | copy-start | bytes 6148
  24.5 46.6 %copy-start.83 = (f32[1,512]{1,0:T(1,128)}, f32[1,512]{1,0:T(1,128)S(1)}, u32[]{:S(2)}) copy-start(f32[1,512]{1,0:T(1,128)S(1)} %get-tuple-element.152) | copy-start | bytes 6148
  24.5 46.6 %copy-start.85 = (f32[1,512]{1,0:T(1,128)}, f32[1,512]{1,0:T(1,128)S(1)}, u32[]{:S(2)}) copy-start(f32[1,512]{1,0:T(1,128)S(1)} %get-tuple-element.153) | copy-start | bytes 6148
  24.5 46.6 %copy-start.87 = (f32[1,512]{1,0:T(1,128)}, f32[1,512]{1,0:T(1,128)S(1)}, u32[]{:S(2)}) copy-start(f32[1,512]{1,0:T(1,128)S(1)} %get-tuple-element.154) | copy-start | bytes 6148
  24.5 46.6 %copy-start.89 = (f32[1,512]{1,0:T(1,128)}, f32[1,512]{1,0:T(1,128)S(1)}, u32[]{:S(2)}) copy-start(f32[1,512]{1,0:T(1,128)S(1)} %get-tuple-element.155) | copy-start | bytes 6148
  24.5 46.6 %copy-start.91 = (f32[1,512]{1,0:T(1,128)}, f32[1,512]{1,0:T(1,128)S(1)}, u32[]{:S(2)}) copy-start(f32[1,512]{1,0:T(1,128)S(1)} %get-tuple-element.156) | copy-start | bytes 6148
  24.5 145.2 %copy-start.70 = (f32[1,512]{1,0:T(1,128)}, f32[1,512]{1,0:T(1,128)S(1)}, u32[]{:S(2)}) copy-start(f32[1,512]{1,0:T(1,128)S(1)} %get-tuple-element.149) | copy-start | bytes 6148
  26.4 44.6 %copy-start.47 = (f32[4,1024]{1,0:T(4,128)}, f32[4,1024]{1,0:T(4,128)S(1)}, u32[]{:S(2)}) copy-start(f32[4,1024]{1,0:T(4,128)S(1)} %get-tuple-element.190) | copy-start | bytes 49156
  26.4 44.6 %copy-start.49 = (f32[4,1024]{1,0:T(4,128)}, f32[4,1024]{1,0:T(4,128)S(1)}, u32[]{:S(2)}) copy-start(f32[4,1024]{1,0:T(4,128)S(1)} %get-tuple-element.199) | copy-start | bytes 49156
  26.5 168.8 %copy-start.65 = (f32[1,8,4,128]{3,1,2,0:T(8,128)}, f32[1,8,4,128]{3,1,2,0:T(8,128)S(1)}, u32[]{:S(2)}) copy-start(f32[1,8,4,128]{3,1,2,0:T(8,128)S(1)} %copy.48) | copy-start | bytes 49156
  27.1 43.9 %copy-start.51 = (f32[4,1024]{1,0:T(4,128)}, f32[4,1024]{1,0:T(4,128)S(1)}, u32[]{:S(2)}) copy-start(f32[4,1024]{1,0:T(4,128)S(1)} %get-tuple-element.194) | copy-start | bytes 49156
  27.2 43.9 %copy-start.53 = (f32[4,1024]{1,0:T(4,128)}, f32[4,1024]{1,0:T(4,128)S(1)}, u32[]{:S(2)}) copy-start(f32[4,1024]{1,0:T(4,128)S(1)} %get-tuple-element.201) | copy-start | bytes 49156
  153.6 16.2 %copy-start = (f32[4,1024,512]{2,1,0:T(8,128)}, f32[4,1024,512]{2,1,0:T(8,128)S(1)}, u32[]{:S(2)}) copy-start(f32[4,1024,512]{2,1,0:T(8,128)S(1)} %get-tuple-element.160) | copy-start | bytes 25165828
  153.6 16.2 %copy-start.1 = (f32[4,1024,512]{2,1,0:T(8,128)}, f32[4,1024,512]{2,1,0:T(8,128)S(1)}, u32[]{:S(2)}) copy-start(f32[4,1024,512]{2,1,0:T(8,128)S(1)} %get-tuple-element.117) | copy-start | bytes 25165828
  153.7 16.1 %copy-start.41 = (f32[4,1024]{1,0:T(4,128)}, f32[4,1024]{1,0:T(4,128)S(1)}, u32[]{:S(2)}) copy-start(f32[4,1024]{1,0:T(4,128)S(1)} %broadcast_multiply_fusion.11) | copy-start | bytes 49156
  153.7 16.1 %copy-start.39 = (f32[4,1024]{1,0:T(4,128)}, f32[4,1024]{1,0:T(4,128)S(1)}, u32[]{:S(2)}) copy-start(f32[4,1024]{1,0:T(4,128)S(1)} %broadcast_multiply_fusion.10) | copy-start | bytes 49156
  153.7 16.1 %copy-start.43 = (f32[4,1024]{1,0:T(4,128)}, f32[4,1024]{1,0:T(4,128)S(1)}, u32[]{:S(2)}) copy-start(f32[4,1024]{1,0:T(4,128)S(1)} %broadcast_multiply_fusion.9) | copy-start | bytes 49156
  153.7 16.1 %copy-start.45 = (f32[4,1024]{1,0:T(4,128)}, f32[4,1024]{1,0:T(4,128)S(1)}, u32[]{:S(2)}) copy-start(f32[4,1024]{1,0:T(4,128)S(1)} %broadcast_multiply_fusion.8) | copy-start | bytes 49156
  178.5 16.7 %slice-start = ((s8[16777216]{0:T(1024)(128)(4,1)}), s8[4194304]{0:T(1024)(128)(4,1)S(1)}, s32[]{:S(2)}) async-start(s8[16777216]{0:T(1024)(128)(4,1)} %bitcast.261), calls=%async_computation.7 | async-start | bytes 8388608
  254.6 48.2 %reduce-scatter.10.cloned.1.call-start = ((), (), s32[]{:S(2)}) async-start(), calls=%async_computation.3 | async-start | bytes 327680
  264.8 429.3 %all-reduce.11.cloned.1.call-start = ((), (), s32[]{:S(2)}) async-start(), calls=%async_computation.6 | async-start | bytes 67108864 | tf_op jit(solution)/shard_map/psum | solution.py:100
  291.2 402.9 %copy-start.42 = (f32[4,1024]{1,0:T(4,128)S(1)}, f32[4,1024]{1,0:T(4,128)}, u32[]{:S(2)}) copy-start(f32[4,1024]{1,0:T(4,128)} %copy-done.41) | copy-start | bytes 49156
  291.2 402.9 %copy-start.44 = (f32[4,1024]{1,0:T(4,128)S(1)}, f32[4,1024]{1,0:T(4,128)}, u32[]{:S(2)}) copy-start(f32[4,1024]{1,0:T(4,128)} %copy-done.43) | copy-start | bytes 49156
  291.2 402.9 %copy-start.60 = (f32[4,1024]{1,0:T(4,128)S(1)}, f32[4,1024]{1,0:T(4,128)}, u32[]{:S(2)}) copy-start(f32[4,1024]{1,0:T(4,128)} %copy-done.59) | copy-start | bytes 49156
  291.2 402.9 %copy-start.62 = (f32[4,1024]{1,0:T(4,128)S(1)}, f32[4,1024]{1,0:T(4,128)}, u32[]{:S(2)}) copy-start(f32[4,1024]{1,0:T(4,128)} %copy-done.61) | copy-start | bytes 49156
  291.2 402.9 %copy-start.71 = (f32[1,512]{1,0:T(1,128)S(1)}, f32[1,512]{1,0:T(1,128)}, u32[]{:S(2)}) copy-start(f32[1,512]{1,0:T(1,128)} %copy-done.70) | copy-start | bytes 6148
  291.2 732.2 %reduce-scatter.14.cloned.1.call-start = ((), (), s32[]{:S(2)}) async-start(), calls=%async_computation.5 | async-start | bytes 163840
  714.7 40.6 %copy-start.46 = (f32[4,1024]{1,0:T(4,128)S(1)}, f32[4,1024]{1,0:T(4,128)}, u32[]{:S(2)}) copy-start(f32[4,1024]{1,0:T(4,128)} %copy-done.45) | copy-start | bytes 49156
  714.7 40.6 %copy-start.64 = (f32[4,1024]{1,0:T(4,128)S(1)}, f32[4,1024]{1,0:T(4,128)}, u32[]{:S(2)}) copy-start(f32[4,1024]{1,0:T(4,128)} %copy-done.63) | copy-start | bytes 49156
  755.4 42.4 %copy-start.4 = (bf16[4096,512]{1,0:T(8,128)(2,1)S(1)}, bf16[4096,512]{1,0:T(8,128)(2,1)}, u32[]{:S(2)}) copy-start(bf16[4096,512]{1,0:T(8,128)(2,1)} %get-tuple-element.84) | copy-start | bytes 12582916
  797.8 28.2 %copy-start.48 = (f32[4,1024]{1,0:T(4,128)S(1)}, f32[4,1024]{1,0:T(4,128)}, u32[]{:S(2)}) copy-start(f32[4,1024]{1,0:T(4,128)} %copy-done.47) | copy-start | bytes 49156
  797.8 28.2 %copy-start.50 = (f32[4,1024]{1,0:T(4,128)S(1)}, f32[4,1024]{1,0:T(4,128)}, u32[]{:S(2)}) copy-start(f32[4,1024]{1,0:T(4,128)} %copy-done.49) | copy-start | bytes 49156
  797.8 28.2 %copy-start.52 = (f32[4,1024]{1,0:T(4,128)S(1)}, f32[4,1024]{1,0:T(4,128)}, u32[]{:S(2)}) copy-start(f32[4,1024]{1,0:T(4,128)} %copy-done.51) | copy-start | bytes 49156
  797.8 28.2 %copy-start.80 = (f32[1,512]{1,0:T(1,128)S(1)}, f32[1,512]{1,0:T(1,128)}, u32[]{:S(2)}) copy-start(f32[1,512]{1,0:T(1,128)} %copy-done.79) | copy-start | bytes 6148
  797.8 28.2 %copy-start.82 = (f32[1,512]{1,0:T(1,128)S(1)}, f32[1,512]{1,0:T(1,128)}, u32[]{:S(2)}) copy-start(f32[1,512]{1,0:T(1,128)} %copy-done.81) | copy-start | bytes 6148
  797.9 28.2 %copy-start.84 = (f32[1,512]{1,0:T(1,128)S(1)}, f32[1,512]{1,0:T(1,128)}, u32[]{:S(2)}) copy-start(f32[1,512]{1,0:T(1,128)} %copy-done.83) | copy-start | bytes 6148
  797.9 28.2 %copy-start.86 = (f32[1,512]{1,0:T(1,128)S(1)}, f32[1,512]{1,0:T(1,128)}, u32[]{:S(2)}) copy-start(f32[1,512]{1,0:T(1,128)} %copy-done.85) | copy-start | bytes 6148
  797.9 28.2 %copy-start.88 = (f32[1,512]{1,0:T(1,128)S(1)}, f32[1,512]{1,0:T(1,128)}, u32[]{:S(2)}) copy-start(f32[1,512]{1,0:T(1,128)} %copy-done.87) | copy-start | bytes 6148
  797.9 28.2 %copy-start.90 = (f32[1,512]{1,0:T(1,128)S(1)}, f32[1,512]{1,0:T(1,128)}, u32[]{:S(2)}) copy-start(f32[1,512]{1,0:T(1,128)} %copy-done.89) | copy-start | bytes 6148
  797.9 28.2 %copy-start.92 = (f32[1,512]{1,0:T(1,128)S(1)}, f32[1,512]{1,0:T(1,128)}, u32[]{:S(2)}) copy-start(f32[1,512]{1,0:T(1,128)} %copy-done.91) | copy-start | bytes 6148
  826.1 67.0 %copy-start.54 = (f32[4,1024]{1,0:T(4,128)S(1)}, f32[4,1024]{1,0:T(4,128)}, u32[]{:S(2)}) copy-start(f32[4,1024]{1,0:T(4,128)} %copy-done.53) | copy-start | bytes 49156
  952.2 19.5 %copy-start.93 = (f32[1,512]{1,0:T(1,128)S(1)}, f32[1,512]{1,0:T(1,128)}, u32[]{:S(2)}) copy-start(f32[1,512]{1,0:T(1,128)} %get-tuple-element.158) | copy-start | bytes 6148
  999.5 16.9 %copy-start.19 = (bf16[1,4,1024,512]{3,2,1,0:T(8,128)(2,1)S(1)}, bf16[1,4,1024,512]{3,2,1,0:T(8,128)(2,1)}, u32[]{:S(2)}) copy-start(bf16[1,4,1024,512]{3,2,1,0:T(8,128)(2,1)} %get-tuple-element.127) | copy-start | bytes 12582916
  999.5 16.9 %copy-start.20 = (bf16[1,4,1024,512]{3,2,1,0:T(8,128)(2,1)S(1)}, bf16[1,4,1024,512]{3,2,1,0:T(8,128)(2,1)}, u32[]{:S(2)}) copy-start(bf16[1,4,1024,512]{3,2,1,0:T(8,128)(2,1)} %get-tuple-element.128) | copy-start | bytes 12582916
  999.5 16.8 %copy-start.21 = (bf16[1,4,1024,512]{3,2,1,0:T(8,128)(2,1)S(1)}, bf16[1,4,1024,512]{3,2,1,0:T(8,128)(2,1)}, u32[]{:S(2)}) copy-start(bf16[1,4,1024,512]{3,2,1,0:T(8,128)(2,1)} %get-tuple-element.129) | copy-start | bytes 12582916
  999.5 16.8 %copy-start.22 = (bf16[1,4,1024,512]{3,2,1,0:T(8,128)(2,1)S(1)}, bf16[1,4,1024,512]{3,2,1,0:T(8,128)(2,1)}, u32[]{:S(2)}) copy-start(bf16[1,4,1024,512]{3,2,1,0:T(8,128)(2,1)} %get-tuple-element.130) | copy-start | bytes 12582916
  (63 other events, 448.8 us)
Sparse Core Ops, SparseCore 0:
  254.7 18.2 reduce-scatter.11
  275.2 17.8 reduce-scatter.9
  999.6 19.1 reduce-scatter.13
Sparse Core Ops, SparseCore 1:
  291.3 402.7 all-reduce.10
where the time goes:
time: 1040 us; the launch traced here: 1030 us
  other arithmetic  462 us (44%)
  waiting for transfers between devices  389 us (37%)
  matrix products  93.3 us (9%)
  blocking collectives  50.9 us (5%)
  local copies, waits for them, and re-layouts  20.1 us (2%)
  between operations  17 us (2%)
    psum x1, waiting for transfers between devices, per_device(): lax.psum(partial_out.astype(jnp.bfloat16), 'tensor').astype(jnp.float32)  389 us
    reduce_sum x3, other arithmetic, per_device(): jnp.sum(dconv * padded[:, k:k + length], axis=(0, 1))  118 us
    another operation x3, other arithmetic, per_device(): jnp.stack(back_list, axis=0)  94 us
    reduce_sum x1, other arithmetic, per_device(): mean = jnp.mean(conv, axis=-1, keepdims=True)  82.5 us
    reduce_sum x2, other arithmetic, per_device(): grad_gain = jnp.sum(dnormed * nhat, axis=(0, 1))  58 us
    dot_general x8, matrix products, contract_cols(): lax.dot_general(left, right, (((1,), (1,)), ((), ())), preferred_element_...  52.8 us
    convert_element_type x1, other arithmetic, per_device(): out_list.append(outputs.astype(jnp.bfloat16))  26.7 us
  transfers between devices with their start and end apart: 4, of which 1 were waited for; matrix products, arithmetic and copies ran while one was open for 6% of the time, Pallas kernels for 0%

commit v1 on v0

v1 whole, which is shorter than its diff:
```python
import functools
import math

import jax
import jax.numpy as jnp
import numpy as np
from jax import lax
from jax.experimental import pallas as pl
from jax.experimental.pallas import tpu as pltpu
from jax.sharding import PartitionSpec as P

MESH = pl.DeviceIdType.MESH
BF = jnp.bfloat16
F32 = jnp.float32
MIB = 1 << 20

eps_norm = 1e-06
beta_first = 0.5
beta_second = 0.5
adam_eps = 1e-08
decay_rate = 0.01
step_count = 6

ROOT_HALF = math.sqrt(0.5)
LOG2E = math.log2(math.e)
SLOPE_LOG = math.log2(2.0 / math.sqrt(math.pi))

BLOCK = 256
SUB = 16
LANES = 128
HCHUNK = 256
TILE = 16


def adam_update(weight, first, second, grad, rate):
    first_new = beta_first * first + (1.0 - beta_first) * grad
    second_new = beta_second * second + (1.0 - beta_second) * grad * grad
    first_hat = first_new / (1.0 - beta_first**step_count)
    second_hat = second_new / (1.0 - beta_second**step_count)
    weight_new = weight - rate * (
        first_hat / (jnp.sqrt(second_hat) + adam_eps) + decay_rate * weight
    )
    return (weight_new, first_new, second_new)


def gather_kernel(dp_n, t_n, w_ref, b_ref, c_ref, wg_ref, bg_ref, cg_ref, local_sem, ws, wr, bs, br, cs, cr):
    d = lax.axis_index("dp")
    t = lax.axis_index("tensor")
    rows = w_ref.shape[1]

    def piece(dd, tt):
        return wg_ref.at[dd, :, pl.ds(pl.multiple_of(tt * rows, 16), rows), :]

    barrier = pltpu.get_barrier_semaphore()
    for k in range(1, dp_n):
        pl.semaphore_signal(barrier, inc=1, device_id=(lax.rem(d + k, dp_n), t), device_id_type=MESH)
    for k in range(1, t_n):
        pl.semaphore_signal(barrier, inc=1, device_id=(d, jnp.bitwise_xor(t, k)), device_id_type=MESH)
    own_w = pltpu.make_async_copy(w_ref, piece(d, t), local_sem.at[0])
    own_b = pltpu.make_async_copy(b_ref, bg_ref.at[t], local_sem.at[1])
    own_c = pltpu.make_async_copy(c_ref, cg_ref.at[d], local_sem.at[2])
    own_w.start()
    own_b.start()
    own_c.start()
    pl.semaphore_wait(barrier, dp_n - 1 + t_n - 1)

    copies = []

    def send(src, dst, ssem, rsem, peer):
        copy = pltpu.make_async_remote_copy(
            src_ref=src, dst_ref=dst, send_sem=ssem, recv_sem=rsem, device_id=peer, device_id_type=MESH
        )
        copy.start()
        copies.append(copy)

    def arrived(dst, rsem):
        pltpu.make_async_copy(dst, dst, rsem).wait()

    for k in range(1, dp_n):
        peer = (lax.rem(d + k, dp_n), t)
        send(w_ref, piece(d, t), ws.at[0, k], wr.at[d, t], peer)
        send(c_ref, cg_ref.at[d], cs.at[k], cr.at[d], peer)
    for k in range(1, t_n):
        send(b_ref, bg_ref.at[t], bs.at[k], br.at[t], (d, jnp.bitwise_xor(t, k)))
    own_w.wait()
    own_b.wait()
    own_c.wait()
    sib = (d, jnp.bitwise_xor(t, 1))
    near = [jnp.bitwise_xor(t, 2), jnp.bitwise_xor(t, 4)]
    far = jnp.bitwise_xor(t, 6)
    order = [lax.rem(d + k, dp_n) for k in range(dp_n)]
    for k in range(dp_n):
        dd = order[k]
        if k > 0:
            arrived(piece(dd, t), wr.at[dd, t])
        for side in range(2):
            send(piece(dd, t), piece(dd, t), ws.at[1 + side, k], wr.at[dd, t], (d, near[side]))
        send(piece(dd, t), piece(dd, t), ws.at[3, k], wr.at[dd, t], sib)
    half = dp_n // 2
    for k in range(dp_n):
        dd = order[k]
        for side in range(2):
            arrived(piece(dd, near[side]), wr.at[dd, near[side]])
            if (k < half) == (side == 0):
                send(
                    piece(dd, near[side]),
                    piece(dd, near[side]),
                    ws.at[6, k],
                    wr.at[dd, near[side]],
                    (d, near[1 - side]),
                )
            send(piece(dd, near[side]), piece(dd, near[side]), ws.at[4 + side, k], wr.at[dd, near[side]], sib)
    for k in range(dp_n):
        dd = order[k]
        arrived(piece(dd, far), wr.at[dd, far])
        send(piece(dd, far), piece(dd, far), ws.at[7, k], wr.at[dd, far], sib)
    for k in range(dp_n):
        dd = order[k]
        for x in (1, 3, 5, 7):
            tt = jnp.bitwise_xor(t, x)
            arrived(piece(dd, tt), wr.at[dd, tt])
    for k in range(1, dp_n):
        dd = lax.rem(d + k, dp_n)
        arrived(cg_ref.at[dd], cr.at[dd])
    for k in range(1, t_n):
        tt = jnp.bitwise_xor(t, k)
        arrived(bg_ref.at[tt], br.at[tt])
    for copy in copies:
        copy.wait_send()


def gather_weights(dp_n, t_n, w_own, bias, channel):
    two, rows, width = w_own.shape
    return pl.pallas_call(
        functools.partial(gather_kernel, dp_n, t_n),
        out_shape=(
            jax.ShapeDtypeStruct((dp_n, two, rows * t_n, width), w_own.dtype),
            jax.ShapeDtypeStruct((t_n,) + bias.shape, bias.dtype),
            jax.ShapeDtypeStruct((dp_n,) + channel.shape, channel.dtype),
        ),
        in_specs=[pl.BlockSpec(memory_space=pl.ANY)] * 3,
        out_specs=(pl.BlockSpec(memory_space=pl.ANY),) * 3,
        scratch_shapes=[
            pltpu.SemaphoreType.DMA((3,)),
            pltpu.SemaphoreType.DMA((8, dp_n)),
            pltpu.SemaphoreType.DMA((dp_n, t_n)),
            pltpu.SemaphoreType.DMA((t_n,)),
            pltpu.SemaphoreType.DMA((t_n,)),
            pltpu.SemaphoreType.DMA((dp_n,)),
            pltpu.SemaphoreType.DMA((dp_n,)),
        ],
        compiler_params=pltpu.CompilerParams(collective_id=0, has_side_effects=True),
        name="gather_weights",
    )(w_own, bias, channel)


def dot_nn(a, b):
    return lax.dot_general(a, b, (((1,), (0,)), ((), ())), preferred_element_type=F32)


def dot_nt(a, b):
    return lax.dot_general(a, b, (((1,), (1,)), ((), ())), preferred_element_type=F32)


def split_rows(count, largest):
    step = largest
    while step >= TILE:
        yield step, count - lax.rem(count, 2 * step), lax.rem(lax.div(count, step), 2) == 1
        step //= 2


def block_kernel(grads, first, n, base, n_recv, length, width, hidden, *refs):
    refs = list(refs)
    meta, x_hbm, dy_hbm, w_hbm, chan, bias = refs[:6]
    refs = refs[6:]
    if not first:
        refs = refs[2:]
    received = refs[:n_recv]
    refs = refs[n_recv:]
    o_hbm = refs[:2]
    own_hbm = refs[2:4]
    refs = refs[4:]
    if grads:
        g_out, small_out, gbias_out = refs[:3]
        refs = refs[3:]
    (x_pack, dy_pack, ob_pack, gb_pack, w_e, w_p, xs, ds, nh, rs, nrm, dzs, hid, dpre, zero) = refs[:15]
    in_sem, out_sem, w_sem, recv_sem = refs[15:19]
    if grads:
        gacc, left_t, gb_acc, sm_acc = refs[19:23]
    groups = width // LANES
    R = BLOCK

    clip_of = [meta[base + k] for k in range(n)]
    len_of = [meta[8 + base + k] for k in range(n)]
    off = [jnp.int32(0)]
    for k in range(n):
        off.append(off[k] + lax.div(len_of[k] + 3 + TILE - 1, TILE) * TILE)
    tiles_of = [lax.div(len_of[k] + TILE - 1, TILE) * TILE for k in range(n)]
    nblk = lax.div(off[n] + TILE + R - 1, R)

    def aligned(v):
        return pl.multiple_of(v, TILE)

    w_copies = []
    for g in range(groups):
        w_copies.append(pltpu.make_async_copy(w_hbm.at[g, 0], w_e.at[:, pl.ds(g * LANES, LANES)], w_sem.at[0, g]))
        w_copies.append(pltpu.make_async_copy(w_hbm.at[g, 1], w_p.at[:, pl.ds(g * LANES, LANES)], w_sem.at[1, g]))

    def clip_in(k, act):
        for j, (src, dst) in enumerate(((x_hbm, x_pack), (dy_hbm, dy_pack))):
            for p, (size, start, have) in enumerate(split_rows(tiles_of[k], length)):

                @pl.when(have)
                def _():
                    copy = pltpu.make_async_copy(
                        src.at[clip_of[k], pl.ds(aligned(start), size), :],
                        dst.at[pl.ds(aligned(off[k] + start), size), :],
                        in_sem.at[k, j, p],
                    )
                    act(copy)

    def clip_out(k, act):
        for j, (src, dsts) in enumerate(((ob_pack, (o_hbm[0], own_hbm[0])), (gb_pack, (o_hbm[1], own_hbm[1])))):
            shift = TILE * j
            for which, dst in enumerate(dsts):
                view = dst.at[clip_of[k]] if which == 0 else dst.at[k]
                p = 0
                for size, start, have in split_rows(tiles_of[k], length):

                    @pl.when(have)
                    def _():
                        copy = pltpu.make_async_copy(
                            src.at[pl.ds(aligned(off[k] + shift + start), size), :],
                            view.at[pl.ds(aligned(start), size), :],
                            out_sem.at[k, 2 * j + which, p],
                        )
                        act(copy)

                    p += 1
                rest = length - tiles_of[k]
                for size, start, have in split_rows(rest, length // 2):

                    @pl.when(have)
                    def _():
                        copy = pltpu.make_async_copy(
                            zero.at[pl.ds(0, size), :],
                            view.at[pl.ds(aligned(tiles_of[k] + start), size), :],
                            out_sem.at[k, 2 * j + which, p],
                        )
                        act(copy)

                    p += 1

    def recv_copies():
        for k in range(n_recv // 2):
            pass

    row_id = lax.broadcasted_iota(jnp.int32, (TILE, width), 0)

    def clear_tail(ref, k, shift):
        left = lax.rem(len_of[k], TILE)
        at = aligned(off[k] + len_of[k] - left + shift)

        @pl.when(left > 0)
        def _():
            tile = ref[pl.ds(at, TILE), :].astype(F32)
            ref[pl.ds(at, TILE), :] = jnp.where(row_id < left, tile, 0.0).astype(ref.dtype)

    def clear_gap(ref, k):
        clear_tail(ref, k, 0)
        at = aligned(off[k] + tiles_of[k])

        @pl.when(off[k + 1] > at)
        def _():
            ref[pl.ds(at, TILE), :] = jnp.zeros((TILE, width), ref.dtype)

    for k in range(n):
        clip_in(k, lambda c: c.start())
        if k == 0:
            for copy in w_copies:
                copy.start()
    n_each = n_recv // 2
    recv_list = []
    if n_recv:
        rec_n = received[0].shape[0]
        rec_base = base - 3 - rec_n
        for j in range(2):
            for k in range(rec_n):
                recv_list.append(
                    pltpu.make_async_copy(
                        received[j].at[k], o_hbm[j].at[meta[16 + rec_base + k]], recv_sem.at[j, k]
                    )
                )
        for copy in recv_list:
            copy.start()

    zero[...] = jnp.zeros_like(zero)
    tail = R + 2 * TILE
    @pl.loop(0, tail // TILE)
    def _(s):
        at = aligned(off[n] + s * TILE)
        x_pack[pl.ds(at, TILE), :] = jnp.zeros((TILE, width), BF)
        dy_pack[pl.ds(at, TILE), :] = jnp.zeros((TILE, width), BF)

    xs[...] = jnp.zeros_like(xs)
    ds[...] = jnp.zeros_like(ds)
    if grads:
        gacc[...] = jnp.zeros_like(gacc)
        gb_acc[...] = jnp.zeros_like(gb_acc)
        sm_acc[...] = jnp.zeros_like(sm_acc)
    for copy in w_copies:
        copy.wait()

    inv_c = 1.0 / width

    def lane(g):
        return slice(g * LANES, (g + 1) * LANES)

    @pl.loop(0, nblk)
    def _(i):
        top = pl.multiple_of(i * R, R)
        for k in range(n):

            @pl.when(i == lax.div(jnp.maximum(off[k] - TILE, 0), R))
            def _():
                clip_in(k, lambda c: c.wait())
                clear_gap(x_pack, k)
                clear_gap(dy_pack, k)

        @pl.when(i == 0)
        def _():
            for g in range(groups):
                xs[g, pl.ds(R + TILE, TILE), :] = x_pack[pl.ds(0, TILE), lane(g)].astype(F32)

        for g in range(groups):
            xs[g, pl.ds(0, 2 * TILE), :] = xs[g, pl.ds(R, 2 * TILE), :]
            ds[g, pl.ds(0, 2 * TILE), :] = ds[g, pl.ds(R, 2 * TILE), :]
        for s in range(0, R, SUB):
            for g in range(groups):
                xs[g, pl.ds(2 * TILE + s, SUB), :] = x_pack[pl.ds(top + TILE + s, SUB), lane(g)].astype(F32)

        for s in range(0, R, SUB):
            conv = []
            for g in range(groups):
                acc = xs[g, pl.ds(s + 13, SUB), :] * chan[0:1, lane(g)] + chan[7:8, lane(g)]
                for k in range(1, 7):
                    acc = acc + xs[g, pl.ds(s + 13 + k, SUB), :] * chan[k : k + 1, lane(g)]
                conv.append(acc)
            mean = jnp.sum(sum(conv), axis=-1, keepdims=True) * inv_c
            cent = [v - mean for v in conv]
            var = jnp.sum(sum([v * v for v in cent]), axis=-1, keepdims=True) * inv_c
            inv = lax.rsqrt(var + eps_norm)
            rs[pl.ds(s, SUB), :] = jnp.broadcast_to(inv, (SUB, LANES))
            for g in range(groups):
                nhat = cent[g] * inv
                nh[g, pl.ds(s, SUB), :] = nhat
                gain = chan[8:9, lane(g)] * ROOT_HALF
                shift = chan[9:10, lane(g)] * ROOT_HALF
                nrm[pl.ds(s, SUB), lane(g)] = (nhat * gain + shift).astype(BF)
                dzs[pl.ds(s, SUB), lane(g)] = (
                    dy_pack[pl.ds(top + s, SUB), lane(g)].astype(F32) * chan[11:12, lane(g)]
                ).astype(BF)

        for c in range(hidden // HCHUNK):
            cols = slice(c * HCHUNK, (c + 1) * HCHUNK)
            pre = dot_nt(nrm[...], w_e[cols, :])
            dhid = dot_nt(dzs[...], w_p[cols, :])
            add = bias[0:1, cols] * ROOT_HALF
            for s in range(0, R, SUB):
                u = pre[s : s + SUB] + add
                v = 1.0 + lax.erf(u)
                hid[pl.ds(s, SUB), cols] = (u * v).astype(BF)
                e = jnp.exp2(SLOPE_LOG - LOG2E * (u * u))
                dp2 = dhid[s : s + SUB] * (v + u * e)
                dpre[pl.ds(s, SUB), cols] = dp2.astype(BF)
                if grads:
                    gb_acc[:, cols] += dp2[0:8] + dp2[8:16]
        branch = dot_nn(hid[...], w_p[...])
        dn2 = dot_nn(dpre[...], w_e[...])

        for s in range(0, R, SUB):
            dn, prod = [], []
            for g in range(groups):
                br = branch[s : s + SUB, lane(g)]
                scale = chan[11:12, lane(g)]
                x_mid = xs[g, pl.ds(s + TILE, SUB), :]
                ob = x_mid + (br * (scale * ROOT_HALF) + scale * chan[10:11, lane(g)])
                ob_pack[pl.ds(top + s, SUB), lane(g)] = ob.astype(BF)
                d2 = dn2[s : s + SUB, lane(g)]
                nhat = nh[g, pl.ds(s, SUB), :]
                half_gain = chan[8:9, lane(g)] * 0.5
                dn.append(d2 * half_gain)
                if grads:
                    p2 = d2 * nhat
                    prod.append(p2 * half_gain)
                    dyf = dy_pack[pl.ds(top + s, SUB), lane(g)].astype(F32)
                    dyb = dyf * br
                    sm_acc[g, 8] += p2[0:8] + p2[8:16]
                    sm_acc[g, 9] += d2[0:8] + d2[8:16]
                    sm_acc[g, 10] += dyf[0:8] + dyf[8:16]
                    sm_acc[g, 11] += dyb[0:8] + dyb[8:16]
                else:
                    prod.append((d2 * nhat) * half_gain)
            m1 = jnp.sum(sum(dn), axis=-1, keepdims=True) * inv_c
            m2 = jnp.sum(sum(prod), axis=-1, keepdims=True) * inv_c
            inv = rs[pl.ds(s, SUB), :]
            for g in range(groups):
                nhat = nh[g, pl.ds(s, SUB), :]
                dconv = inv * (dn[g] - m1 - nhat * m2)
                ds[g, pl.ds(2 * TILE + s, SUB), :] = dconv
                if grads:
                    sm_acc[g, 7] += dconv[0:8] + dconv[8:16]
                    for k in range(7):
                        tp = dconv * xs[g, pl.ds(s + 13 + k, SUB), :]
                        sm_acc[g, k] += tp[0:8] + tp[8:16]

        for s in range(0, R, SUB):
            for g in range(groups):
                acc = ds[g, pl.ds(s + 19, SUB), :] * chan[0:1, lane(g)]
                for k in range(1, 7):
                    acc = acc + ds[g, pl.ds(s + 19 - k, SUB), :] * chan[k : k + 1, lane(g)]
                if s == 0:
                    back_at = jnp.maximum(top - TILE, 0)
                else:
                    back_at = top + s - TILE
                dyf = dy_pack[pl.ds(aligned(back_at), SUB), lane(g)].astype(F32)
                gb_pack[pl.ds(top + s, SUB), lane(g)] = (dyf + acc).astype(BF)

        if grads:
            for which, (left, right) in enumerate(((nrm, dpre), (dzs, hid))):
                left_t[...] = left[...].T
                for c in range(hidden // HCHUNK):
                    cols = slice(c * HCHUNK, (c + 1) * HCHUNK)
                    gacc[which, :, cols] += dot_nn(left_t[...], right[:, cols])

        for k in range(n):

            @pl.when(i == lax.div(off[k] + len_of[k] + TILE - 1, R))
            def _():
                clear_tail(ob_pack, k, 0)
                clear_tail(gb_pack, k, TILE)
                clip_out(k, lambda c: c.start())

    if grads:
        for which in range(2):
            for c in range(hidden // HCHUNK):
                cols = slice(c * HCHUNK, (c + 1) * HCHUNK)
                g_out[which, cols, :] = (gacc[which, :, cols] * ROOT_HALF).T.astype(BF)
        gbias_out[...] = jnp.sum(gb_acc[...], axis=0, keepdims=True) * 0.5
        for g in range(groups):
            for k in range(12):
                small_out[k : k + 1, lane(g)] = jnp.sum(sm_acc[g, k], axis=0, keepdims=True)
    for k in range(n):
        clip_out(k, lambda c: c.wait())
    for copy in recv_list:
        copy.wait()


def run_block(grads, n, base, meta, x, dy, w, chan, bias, held, received):
    clips, length, width = x.shape
    hidden = w.shape[2]
    groups = width // LANES
    first = held is None
    R = BLOCK
    rows = n * (length + TILE) + 2 * R + 2 * TILE
    out_shape = [jax.ShapeDtypeStruct((clips, length, width), BF)] * 2 + [
        jax.ShapeDtypeStruct((n, length, width), BF)
    ] * 2
    any_spec = pl.BlockSpec(memory_space=pl.ANY)
    vmem_spec = pl.BlockSpec(memory_space=pltpu.VMEM)
    out_specs = [any_spec] * 4
    if grads:
        out_shape += [
            jax.ShapeDtypeStruct((2, hidden, width), BF),
            jax.ShapeDtypeStruct((12, width), F32),
            jax.ShapeDtypeStruct((1, hidden), F32),
        ]
        out_specs += [vmem_spec] * 3
    args = [meta, x, dy, w, chan, bias]
    in_specs = [
        pl.BlockSpec(memory_space=pltpu.SMEM),
        any_spec,
        any_spec,
        any_spec,
        vmem_spec,
        vmem_spec,
    ]
    aliases = {}
    if not first:
        aliases = {6: 0, 7: 1}
        args += list(held)
        in_specs += [any_spec] * 2
    args += list(received)
    in_specs += [any_spec] * len(received)
    scratch = [
        pltpu.VMEM((rows, width), BF),
        pltpu.VMEM((rows, width), BF),
        pltpu.VMEM((rows, width), BF),
        pltpu.VMEM((rows, width), BF),
        pltpu.VMEM((hidden, width), BF),
        pltpu.VMEM((hidden, width), BF),
        pltpu.VMEM((groups, R + 2 * TILE, LANES), F32),
        pltpu.VMEM((groups, R + 2 * TILE, LANES), F32),
        pltpu.VMEM((groups, R, LANES), F32),
        pltpu.VMEM((R, LANES), F32),
        pltpu.VMEM((R, width), BF),
        pltpu.VMEM((R, width), BF),
        pltpu.VMEM((R, hidden), BF),
        pltpu.VMEM((R, hidden), BF),
        pltpu.VMEM((length // 2, width), BF),
        pltpu.SemaphoreType.DMA((n, 2, 8)),
        pltpu.SemaphoreType.DMA((n, 4, 16)),
        pltpu.SemaphoreType.DMA((2, groups)),
        pltpu.SemaphoreType.DMA((2, 8)),
    ]
    if grads:
        scratch += [
            pltpu.VMEM((2, width, hidden), F32),
            pltpu.VMEM((width, R), BF),
            pltpu.VMEM((8, hidden), F32),
            pltpu.VMEM((groups, 12, 8, LANES), F32),
        ]
    per_row = 2 * width * hidden * (6 if grads else 4)
    cost = pl.CostEstimate(
        flops=int(per_row * n * length * 1.5), bytes_accessed=n * length * width * 12, transcendentals=0
    )
    return pl.pallas_call(
        functools.partial(block_kernel, grads, first, n, base, len(received), length, width, hidden),
        out_shape=tuple(out_shape),
        in_specs=in_specs,
        out_specs=tuple(out_specs),
        scratch_shapes=scratch,
        input_output_aliases=aliases,
        cost_estimate=cost,
        compiler_params=pltpu.CompilerParams(vmem_limit_bytes=56 * MIB),
        name="block_grads" if grads else "block_plain",
    )(*args)


def place_kernel(base, counts, meta, *refs):
    n_in = 2 + 2 * len(counts)
    ins = refs[2:n_in]
    outs = refs[n_in : n_in + 2]
    sem = refs[n_in + 2]
    copies = []
    at = base
    for block, count in enumerate(counts):
        for j in range(2):
            for k in range(count):
                copies.append(
                    pltpu.make_async_copy(
                        ins[2 * block + j].at[k], outs[j].at[meta[16 + at + k]], sem.at[j, at - base + k]
                    )
                )
        at += count
    for copy in copies:
        copy.start()
    for copy in copies:
        copy.wait()


def place_received(base, counts, meta, held, arrays):
    any_spec = pl.BlockSpec(memory_space=pl.ANY)
    return pl.pallas_call(
        functools.partial(place_kernel, base, counts),
        out_shape=tuple(jax.ShapeDtypeStruct(h.shape, h.dtype) for h in held),
        in_specs=[pl.BlockSpec(memory_space=pltpu.SMEM)] + [any_spec] * (2 + len(arrays)),
        out_specs=(any_spec,) * 2,
        scratch_shapes=[pltpu.SemaphoreType.DMA((2, sum(counts)))],
        input_output_aliases={1: 0, 2: 1},
        name="place_received",
    )(meta, *held, *arrays)


def swap(value, axis, size, bit):
    return lax.ppermute(value, axis, [(i, i ^ bit) for i in range(size)])


def take_bit(index, bit):
    return lax.rem(lax.div(index, bit), 2)


def halve(value, dim, keep):
    half = value.shape[dim] // 2
    mine = lax.dynamic_slice_in_dim(value, keep * half, half, dim)
    other = lax.dynamic_slice_in_dim(value, (1 - keep) * half, half, dim)
    return mine, other


def fold(value, dim, axis, size, bit):
    keep = take_bit(lax.axis_index(axis), bit)
    mine, other = halve(value, dim, keep)
    got = swap(other, axis, size, bit)
    return (mine.astype(F32) + got.astype(F32)).astype(BF)


def per_device(
    frames,
    cotangent,
    lengths,
    expand_weight,
    expand_first,
    expand_second,
    project_weight,
    project_first,
    project_second,
    hidden_bias,
    hidden_bias_first,
    hidden_bias_second,
    channel_param,
    channel_first,
    channel_second,
    *,
    dp_n,
    t_n,
):
    micro, clips, length, width = frames.shape
    hidden_part = expand_weight.shape[1]
    hidden = hidden_part * t_n
    width_part = expand_weight.shape[0]
    count = micro * clips
    d = lax.axis_index("dp")
    t = lax.axis_index("tensor")

    lens = lengths.reshape(count)
    ids = jnp.arange(count, dtype=jnp.int32)
    ahead = (lens[None, :] > lens[:, None]) | ((lens[None, :] == lens[:, None]) & (ids[None, :] < ids[:, None]))
    rank = jnp.sum(ahead.astype(jnp.int32), axis=1)
    per_core = count // 2
    table = np.zeros((t_n, per_core), np.int32)
    for tt in range(t_n):
        core, chip = tt % 2, tt // 2
        own = [4 * (j // 2) + (3 * (j % 2) if core == 0 else 1 + (j % 2)) for j in range(per_core)]
        pair = [chip, per_core - 1 - chip]
        table[tt] = [own[j] for j in pair] + [own[j] for j in range(per_core) if j not in pair]
    both = np.concatenate([table, table[np.arange(t_n) ^ 1]], axis=1)
    wanted = lax.dynamic_slice_in_dim(jnp.asarray(both), t, 1, 0).reshape(2 * per_core)
    hit = (rank[None, :] == wanted[:, None]).astype(jnp.int32)
    seq = jnp.sum(hit * ids[None, :], axis=1)
    seq_len = jnp.sum(hit * lens[None, :], axis=1)
    meta = jnp.concatenate([seq[:per_core], seq_len[:per_core], seq[per_core:]])

    w_own = jnp.stack([expand_weight.T.astype(BF), project_weight.astype(BF)])
    w_all, bias_all, chan_all = gather_weights(dp_n, t_n, w_own, hidden_bias.reshape(1, hidden_part), channel_param)
    if width_part != LANES:
        w_all = jnp.transpose(w_all, (1, 2, 0, 3)).reshape(2, hidden, width // LANES, LANES)
        w_all = jnp.transpose(w_all, (2, 0, 1, 3))
    bias = bias_all.reshape(1, hidden)
    chan = jnp.transpose(chan_all, (1, 0, 2)).reshape(12, width)

    x = frames.reshape(count, length, width)
    dy = cotangent.reshape(count, length, width)
    calls = [(True, 2), (False, 3), (False, 3)]
    held = None
    base = 0
    pending = []
    for index, (grads, n) in enumerate(calls):
        received = pending[0] if index == 2 else ()
        outs = run_block(grads, n, base, meta, x, dy, w_all, chan, bias, held, received)
        held = outs[:2]
        pending.append(tuple(swap(o, "tensor", t_n, 1) for o in outs[2:4]))
        if grads:
            g_part, small_part, gbias_part = outs[4:]
        base += n
    held = place_received(2, [3, 3], meta, held, pending[1] + pending[2])

    g = g_part.reshape(2, t_n // 2, 2, hidden_part, dp_n, width_part)
    g = jnp.transpose(g, (2, 1, 4, 0, 3, 5)) if False else g
    g = fold(g, 2, "tensor", t_n, 1)
    g = fold(g.reshape(2, 2, 2, hidden_part, dp_n, width_part), 2, "tensor", t_n, 2)
    g = fold(g.reshape(2, 2, hidden_part, dp_n, width_part), 1, "tensor", t_n, 4)
    g = g.reshape(2, hidden_part, dp_n, width_part)
    bit = dp_n // 2
    while bit >= 1:
        g = fold(g, 2, "dp", dp_n, bit)
        bit //= 2
    g = g.reshape(2, hidden_part, width_part).astype(F32)
    shard_expand = g[0].T
    shard_project = g[1]

    small = jnp.concatenate([small_part.reshape(12 * width), gbias_part.reshape(hidden)])
    for bit in (1, 2, 4):
        small = small + swap(small, "tensor", t_n, bit)
    bit = 1
    while bit < dp_n:
        small = small + swap(small, "dp", dp_n, bit)
        bit *= 2
    g_small = lax.dynamic_slice_in_dim(small[: 12 * width].reshape(12, width), d * width_part, width_part, 1)
    g_bias = lax.dynamic_slice_in_dim(small[12 * width :], t * hidden_part, hidden_part, 0)
    back_sum = g_small[10]
    shard_channel = jnp.concatenate(
        [
            g_small[0:8],
            g_small[8:10] * 0.5,
            (back_sum * channel_param[11])[None],
            (g_small[11] * ROOT_HALF + back_sum * channel_param[10])[None],
        ],
        axis=0,
    )

    e_new, e_first, e_second = adam_update(expand_weight, expand_first, expand_second, shard_expand, 0.02)
    p_new, p_first, p_second = adam_update(project_weight, project_first, project_second, shard_project, 0.01)
    b_new, b_first, b_second = adam_update(hidden_bias, hidden_bias_first, hidden_bias_second, g_bias, 0.1)
    c_new, c_first, c_second = adam_update(channel_param, channel_first, channel_second, shard_channel, 0.2)
    return (
        held[0].reshape(frames.shape),
        held[1].reshape(frames.shape),
        e_new,
        e_first,
        e_second,
        e_new.astype(BF),
        p_new,
        p_first,
        p_second,
        p_new.astype(BF),
        b_new,
        b_first,
        b_second,
        c_new,
        c_first,
        c_second,
    )


def solution(mesh):
    frame_spec = P(None, "dp", None, None)
    e_spec = P("dp", "tensor")
    p_spec = P("tensor", "dp")
    b_spec = P("tensor")
    c_spec = P(None, "dp")
    in_specs = (
        (frame_spec, frame_spec, P(None, "dp")) + (e_spec,) * 3 + (p_spec,) * 3 + (b_spec,) * 3 + (c_spec,) * 3
    )
    out_specs = (frame_spec, frame_spec) + (e_spec,) * 4 + (p_spec,) * 4 + (b_spec,) * 3 + (c_spec,) * 3
    body = functools.partial(per_device, dp_n=mesh.shape["dp"], t_n=mesh.shape["tensor"])
    return jax.shard_map(body, mesh=mesh, in_specs=in_specs, out_specs=out_specs, check_vma=False)
```

time: 1040 us -> 703 us (0.68)
  Pallas kernels: 0 us -> 624 us
  other arithmetic: 462 us -> 11.5 us
  waiting for transfers between devices: 389 us -> 25.1 us
  matrix products: 93.3 us -> 0 us
  blocking collectives: 50.9 us -> 0 us
  starting transfers between devices: 0.16 us -> 27 us
  between operations: 17 us -> 1.23 us
    pallas_call x0 -> x5, Pallas kernels: none -> 624 us  [the longest x1 383 us: place_received(): pl.pallas_call(functools.partial(place_kernel, base, counts), out_shape=t...]
    psum x1 -> x0, waiting for transfers between devices: 389 us -> none  [per_device(): lax.psum(partial_out.astype(jnp.bfloat16), 'tensor').astype(jnp.float32)]
    reduce_sum x12 -> x2, other arithmetic: 296 us -> 0.37 us  [the longest x1 0.18 us: per_device(): rank = jnp.sum(ahead.astype(jnp.int32), axis=1)]
    another operation x4 -> x3, other arithmetic: 101 us -> 2.45 us  [per_device(): w_own = jnp.stack([expand_weight.T.astype(BF), project_weight.astype(BF)])]
    dot_general x24 -> x0, matrix products: 93.3 us -> none  [the longest x8 52.8 us: contract_cols(): lax.dot_general(left, right, (((1,), (1,)), ((), ())), preferred_element_...]
    convert_element_type x14 -> x7, other arithmetic: 47 us -> 5.24 us  [the longest x4 3.69 us: fold(): return (mine.astype(F32) + got.astype(F32)).astype(BF)]
    all_gather x3 -> x0, blocking collectives: 41.5 us -> none  [the longest x1 15 us: per_device(): channel_full = lax.all_gather(channel_param, 'dp', axis=1, tiled=True)]
    ppermute x0 -> x16, starting transfers between devices: none -> 27 us  [swap(): return lax.ppermute(value, axis, [(i, i ^ bit) for i in range(size)])]
  transfers between devices with their start and end apart: 4 -> 16, of which waited for: 1 -> 4; matrix products, arithmetic and copies ran while one was open for 6% -> 2% of each run, Pallas kernels for 0% -> 26%
where the time goes in v1:
time: 703 us; the launch traced here: 704 us
  Pallas kernels  624 us (89%)
  starting transfers between devices  27 us (4%)
  waiting for transfers between devices  25.1 us (4%)
  local copies, waits for them, and re-layouts  14.6 us (2%)
  other arithmetic  11.5 us (2%)
    pallas_call x1, Pallas kernels, place_received(): pl.pallas_call(functools.partial(place_kernel, base, counts), out_shape=t...  383 us
    pallas_call x3, Pallas kernels, run_block(): pl.pallas_call(functools.partial(block_kernel, grads, first, n, base, len...  213 us
    pallas_call x1, Pallas kernels, gather_weights(): pl.pallas_call(functools.partial(gather_kernel, dp_n, t_n), out_shape=(ja...  27.9 us
    ppermute x16, starting transfers between devices, swap(): return lax.ppermute(value, axis, [(i, i ^ bit) for i in range(size)])  27 us
    ppermute x16, waiting for transfers between devices, swap(): return lax.ppermute(value, axis, [(i, i ^ bit) for i in range(size)])  25.1 us
  transfers between devices with their start and end apart: 16, of which 4 were waited for; matrix products, arithmetic and copies ran while one was open for 2% of the time, Pallas kernels for 26%

profile of v1, /device:TPU:0, one launch (start us, length us, event | category | flops | bytes accessed | tf_op | source)
XLA Modules:
  0.0 703.7 jit_solution(6767303864583444168)
XLA Ops:
  0.7 0.8 gt.15
  1.4 0.2 convert_reduce_fusion
  1.6 0.7 fusion.11
  2.3 0.2 fusion.6
  2.5 0.1 fusion.20
  2.6 0.9 convert_bitcast_fusion.1
  3.5 0.9 convert_bitcast_fusion
  4.4 0.7 pad_maximum_fusion.w_ref
  5.0 27.9 %gather_weights.1 = (bf16[4,2,1536,128]{3,2,1,0:T(8,128)(2,1)}, f32[8,1,192]{2,1,0:T(1,128)}, f32[4,12,128]{2,1,0:T(8,128)}) custom-call(bf16[2,192,128]{2,1,0:T(8,128)(2,1)} %pad_maximum_fusion.w_ref, f32[1,192]{1,0:T(1,128)} %bitcast.55, f32[12,128]{1,0:T(8,128)} %c_ref.1), custom_call_target="tpu_custom_call" | custom-call | tf_op jit(solution)/shard_map/gather_weights/pallas_call | solution.py:134
  32.9 0.8 copy.42
  33.7 0.6 copy.51
  34.3 0.7 reduce
  35.1 0.7 reshape.110.refs_5_
  35.7 0.6 pad_add_fusion.refs_0_.meta
  36.3 32.4 %block_grads.1 = (bf16[16,1024,512]{2,1,0:T(8,128)(2,1)}, bf16[16,1024,512]{2,1,0:T(8,128)(2,1)}, bf16[2,1024,512]{2,1,0:T(8,128)(2,1)}, bf16[2,1024,512]{2,1,0:...) custom-call(s32[24]{0:T(128)} %pad_add_fusion.refs_0_.meta, ...), custom_call_target="tpu_custom_call" | custom-call | flops 28991029248 | bytes 12582912 | tf_op jit(solution)/shard_map/block_grads/pallas_call | solution.py:527
  68.8 0.7 reduce.1
  69.5 0.8 reshape.115
  70.3 4.0 collective-permute-start.11
  74.3 0.9 collective-permute-done.11
  75.1 0.9 collective-permute-start.12
  76.1 0.4 collective-permute-start.1
  76.6 3.8 reshape.113
  80.3 10.8 %collective-permute-start.13 = (f32[7680]{0:T(1024)S(1)}, f32[7680]{0:T(1024)S(1)}, u32[]{:S(2)}, u32[]{:S(2)}) collective-permute-start(f32[7680]{0:T(1024)S(1)} %add.164), channel_id=1, source_target_pairs={{0,4},{1,5},{2,6},{3,7},{4,0},{5,1},{6,2},{7,3},{8,12},{9,13},{10,... | collective-permute-start | bytes 92168 | tf_op jit(solution)/shard_map/ppermute | solution.py:576
  91.1 2.3 constant_dynamic-slice_fusion.5
  93.5 0.4 copy.48
  94.0 49.4 %block_plain.2 = (bf16[16,1024,512]{2,1,0:T(8,128)(2,1)}, bf16[16,1024,512]{2,1,0:T(8,128)(2,1)}, bf16[3,1024,512]{2,1,0:T(8,128)(2,1)}, bf16[3,1024,512]{2,1,0:T(8,128)(2,1)}) custom-call(s32[24]{0:T(128)} %pad_add_fusion.refs_0_.meta, bf16[16,1024,512]{2,1,0:T(8,128)(2,1)} %bitcast.58, ...), custom_call_target="tpu_custom_call", output_to_operand_aliasing={{0}: (6, {}), {1}: (7, {})} | custom-call | flops 28991029248 | bytes 18874368 | tf_op jit(solution)/shard_map/block_plain/pallas_call | solution.py:527
  143.5 0.5 collective-permute-start.3
  144.0 8.0 %collective-permute-start.15 = (f32[7680]{0:T(1024)S(1)}, f32[7680]{0:T(1024)S(1)}, u32[]{:S(2)}, u32[]{:S(2)}) collective-permute-start(f32[7680]{0:T(1024)S(1)} %add.166), channel_id=1, source_target_pairs={{0,16},{8,24},{16,0},{24,8},{1,17},{9,25},{17,1},{25,9},{2,18},{10... | collective-permute-start | bytes 92168 | tf_op jit(solution)/shard_map/ppermute | solution.py:576
  152.0 1.8 add_convert_fusion
  153.8 1.0 constant_dynamic-slice_fusion.3
  154.8 1.0 copy.50
  155.9 131.5 %block_plain.3 = (bf16[16,1024,512]{2,1,0:T(8,128)(2,1)}, bf16[16,1024,512]{2,1,0:T(8,128)(2,1)}, bf16[3,1024,512]{2,1,0:T(8,128)(2,1)}, bf16[3,1024,512]{2,1,0:T(8,128)(2,1)}) custom-call(s32[24]{0:T(128)} %pad_add_fusion.refs_0_.meta, bf16[16,1024,512]{2,1,0:T(8,128)(2,1)} %bitcast.59, ...), custom_call_target="tpu_custom_call", output_to_operand_aliasing={{0}: (6, {}), {1}: (7, {})} | custom-call | flops 28991029248 | bytes 18874368 | tf_op jit(solution)/shard_map/block_plain/pallas_call | solution.py:527
  287.5 0.2 collective-permute-start.4
  287.6 0.4 collective-permute-start.5
  288.1 1.7 add_convert_fusion.1
  289.9 1.1 collective-permute-start.8
  291.0 0.1 slice_multiply_fusion
  291.1 10.0 %collective-permute-done.8 = bf16[2,1,192,4,128]{4,2,3,0,1:T(8,128)(2,1)S(1)} collective-permute-done((bf16[2,1,192,4,128]{4,2,3,0,1:T(8,128)(2,1)S(1)}, bf16[2,1,192,4,128]{4,2,3,0,1:T(8,128)(2,1)S(1)}, u32[]{:S(2)}, u32[]{:S(2)}) %collective-permute-start.8) | collective-permute-done | bytes 393248 | tf_op jit(solution)/shard_map/ppermute | solution.py:576
  301.1 0.1 fusion
  301.2 0.3 collective-permute-start.9
  301.6 0.6 multiply_subtract_fusion.2
  302.2 10.3 %collective-permute-done.9 = bf16[2,192,2,128]{3,1,2,0:T(8,128)(2,1)S(1)} collective-permute-done((bf16[2,192,2,128]{3,1,2,0:T(8,128)(2,1)S(1)}, bf16[2,192,2,128]{3,1,2,0:T(8,128)(2,1)S(1)}, u32[]{:S(2)}, u32[]{:S(2)}) %collective-permute-start.9) | collective-permute-done | bytes 196640 | tf_op jit(solution)/shard_map/ppermute | solution.py:576
  312.7 0.7 multiply_subtract_fusion.3
  313.3 3.9 collective-permute-done.10
  317.3 0.8 fusion.16
  318.1 0.8 fusion.18
  318.9 1.6 copy-done.1
  320.5 383.0 %place_received.1 = (bf16[16,1024,512]{2,1,0:T(8,128)(2,1)}, bf16[16,1024,512]{2,1,0:T(8,128)(2,1)}) custom-call(s32[24]{0:T(128)} %pad_add_fusion.refs_0_.meta, bf16[16,1024,512]{2,1,0:T(8,128)(2,1)} %get-tuple-element.45.refs_0_, bf16[16,1024,512]{2,1,0:T(8,128)(2,1)} %get-tuple-element.46.refs_1_, ...), custom_call_target="tpu_custom_call", output_to_operand_aliasing={{0}: (1, {}), {1}: (2, {})} | custom-call | tf_op jit(solution)/shard_map/place_received/pallas_call | solution.py:564
  (62 shorter events, 0.8 us)
Async XLA Ops:
  70.3 4.9 collective-permute-start.11
  75.1 5.2 collective-permute-start.12
  76.0 79.7 %collective-permute-start = (bf16[2,1024,512]{2,1,0:T(8,128)(2,1)}, bf16[2,1024,512]{2,1,0:T(8,128)(2,1)}, u32[]{:S(2)}, u32[]{:S(2)}) collective-permute-start(bf16[2,1024,512]{2,1,0:T(8,128)(2,1)} %get-tuple-element.43), channel_id=1, source_target_pairs={{0,1},{1,0},{2,3},{3,2},{4,5},{5,4},{6,7},{7,6},{8,9},{9,8},{10,11... | collective-permute-start | bytes 6291464 | tf_op jit(solution)/shard_map/ppermute | solution.py:576
  76.1 79.8 %collective-permute-start.1 = (bf16[2,1024,512]{2,1,0:T(8,128)(2,1)}, bf16[2,1024,512]{2,1,0:T(8,128)(2,1)}, u32[]{:S(2)}, u32[]{:S(2)}) collective-permute-start(bf16[2,1024,512]{2,1,0:T(8,128)(2,1)} %get-tuple-element.44), channel_id=1, source_target_pairs={{0,1},{1,0},{2,3},{3,2},{4,5},{5,4},{6,7},{7,6},{8,9},{9,8},{10,11... | collective-permute-start | bytes 6291464 | tf_op jit(solution)/shard_map/ppermute | solution.py:576
  80.3 13.6 %collective-permute-start.13 = (f32[7680]{0:T(1024)S(1)}, f32[7680]{0:T(1024)S(1)}, u32[]{:S(2)}, u32[]{:S(2)}) collective-permute-start(f32[7680]{0:T(1024)S(1)} %add.164), channel_id=1, source_target_pairs={{0,4},{1,5},{2,6},{3,7},{4,0},{5,1},{6,2},{7,3},{8,12},{9,13},{10,... | collective-permute-start | bytes 92168 | tf_op jit(solution)/shard_map/ppermute | solution.py:576
  93.8 50.1 %collective-permute-start.6 = (bf16[2,4,1,192,4,128]{5,3,4,2,1,0:T(8,128)(2,1)S(1)}, bf16[2,4,1,192,4,128]{5,3,4,2,1,0:T(8,128)(2,1)}, u32[]{:S(2)}, u32[]{:S(2)}) collective-permute-start(bf16[2,4,1,192,4,128]{5,3,4,2,1,0:T(8,128)(2,1)S(1)} %copy.48), channel_id=1, source_target_pairs={{0,1},{1,0},{2,3},{3,2},{4,5},{5,4},{6,7},{7,6},{8,9},{9,8},{10,11... | collective-permute-start | bytes 4718600 | tf_op jit(solution)/shard_map/ppermute | solution.py:576
  93.9 49.6 %collective-permute-start.14 = (f32[7680]{0:T(1024)S(1)}, f32[7680]{0:T(1024)S(1)}, u32[]{:S(2)}, u32[]{:S(2)}) collective-permute-start(f32[7680]{0:T(1024)S(1)} %add.165), channel_id=1, source_target_pairs={{0,8},{8,0},{16,24},{24,16},{1,9},{9,1},{17,25},{25,17},{2,10},{10... | collective-permute-start | bytes 92168 | tf_op jit(solution)/shard_map/ppermute | solution.py:576
  94.0 58.0 %copy-start = (bf16[2,4,1,192,4,128]{5,4,3,2,1,0:T(4,128)(2,1)S(1)}, bf16[2,4,1,192,4,128]{5,4,3,2,1,0:T(4,128)(2,1)}, u32[]{:S(2)}) copy-start(bf16[2,4,1,192,4,128]{5,4,3,2,1,0:T(4,128)(2,1)} %get-tuple-element.72) | copy-start | bytes 4718596
  143.4 175.4 %collective-permute-start.2 = (bf16[3,1024,512]{2,1,0:T(8,128)(2,1)}, bf16[3,1024,512]{2,1,0:T(8,128)(2,1)}, u32[]{:S(2)}, u32[]{:S(2)}) collective-permute-start(bf16[3,1024,512]{2,1,0:T(8,128)(2,1)} %get-tuple-element.47), channel_id=1, source_target_pairs={{0,1},{1,0},{2,3},{3,2},{4,5},{5,4},{6,7},{7,6},{8,9},{9,8},{10,11... | collective-permute-start | bytes 9437192 | tf_op jit(solution)/shard_map/ppermute | solution.py:576
  143.5 175.3 %collective-permute-start.3 = (bf16[3,1024,512]{2,1,0:T(8,128)(2,1)}, bf16[3,1024,512]{2,1,0:T(8,128)(2,1)}, u32[]{:S(2)}, u32[]{:S(2)}) collective-permute-start(bf16[3,1024,512]{2,1,0:T(8,128)(2,1)} %get-tuple-element.48), channel_id=1, source_target_pairs={{0,1},{1,0},{2,3},{3,2},{4,5},{5,4},{6,7},{7,6},{8,9},{9,8},{10,11... | collective-permute-start | bytes 9437192 | tf_op jit(solution)/shard_map/ppermute | solution.py:576
  144.0 143.6 %collective-permute-start.15 = (f32[7680]{0:T(1024)S(1)}, f32[7680]{0:T(1024)S(1)}, u32[]{:S(2)}, u32[]{:S(2)}) collective-permute-start(f32[7680]{0:T(1024)S(1)} %add.166), channel_id=1, source_target_pairs={{0,16},{8,24},{16,0},{24,8},{1,17},{9,25},{17,1},{25,9},{2,18},{10... | collective-permute-start | bytes 92168 | tf_op jit(solution)/shard_map/ppermute | solution.py:576
  155.8 132.3 %collective-permute-start.7 = (bf16[2,2,1,192,4,128]{5,3,4,0,2,1:T(8,128)(2,1)}, bf16[2,2,1,192,4,128]{5,3,4,0,2,1:T(8,128)(2,1)}, u32[]{:S(2)}, u32[]{:S(2)}) collective-permute-start(bf16[2,2,1,192,4,128]{5,3,4,0,2,1:T(8,128)(2,1)} %copy.50), channel_id=1, source_target_pairs={{0,2},{1,3},{2,0},{3,1},{4,6},{5,7},{6,4},{7,5},{8,10},{9,11},{10,... | collective-permute-start | bytes 2359304 | tf_op jit(solution)/shard_map/ppermute | solution.py:576
  287.4 3.6 copy-start.8
  287.4 14.2 %copy-start.9 = (f32[12,128]{1,0:T(8,128)S(1)}, f32[12,128]{1,0:T(8,128)}, u32[]{:S(2)}) copy-start(f32[12,128]{1,0:T(8,128)} %param.29) | copy-start | bytes 18436
  287.4 14.2 %copy-start.10 = (f32[12,128]{1,0:T(8,128)S(1)}, f32[12,128]{1,0:T(8,128)}, u32[]{:S(2)}) copy-start(f32[12,128]{1,0:T(8,128)} %param.30) | copy-start | bytes 18436
  287.4 25.2 %copy-start.11 = (f32[192]{0:T(256)S(1)}, f32[192]{0:T(256)}, u32[]{:S(2)}) copy-start(f32[192]{0:T(256)} %param.25) | copy-start | bytes 2308
  287.4 25.2 %copy-start.12 = (f32[192]{0:T(256)S(1)}, f32[192]{0:T(256)}, u32[]{:S(2)}) copy-start(f32[192]{0:T(256)} %param.26) | copy-start | bytes 2308
  287.5 25.2 %copy-start.13 = (f32[192]{0:T(256)S(1)}, f32[192]{0:T(256)}, u32[]{:S(2)}) copy-start(f32[192]{0:T(256)} %param.27) | copy-start | bytes 2308
  287.5 31.4 %collective-permute-start.4 = (bf16[3,1024,512]{2,1,0:T(8,128)(2,1)}, bf16[3,1024,512]{2,1,0:T(8,128)(2,1)S(1)}, u32[]{:S(2)}, u32[]{:S(2)}) collective-permute-start(bf16[3,1024,512]{2,1,0:T(8,128)(2,1)} %get-tuple-element.49), channel_id=1, source_target_pairs={{0,1},{1,0},{2,3},{3,2},{4,5},{5,4},{6,7},{7,6},{8,9},{9,8},{10,11... | collective-permute-start | bytes 9437192 | tf_op jit(solution)/shard_map/ppermute | solution.py:576
  287.6 31.2 %collective-permute-start.5 = (bf16[3,1024,512]{2,1,0:T(8,128)(2,1)}, bf16[3,1024,512]{2,1,0:T(8,128)(2,1)}, u32[]{:S(2)}, u32[]{:S(2)}) collective-permute-start(bf16[3,1024,512]{2,1,0:T(8,128)(2,1)} %get-tuple-element.50), channel_id=1, source_target_pairs={{0,1},{1,0},{2,3},{3,2},{4,5},{5,4},{6,7},{7,6},{8,9},{9,8},{10,11... | collective-permute-start | bytes 9437192 | tf_op jit(solution)/shard_map/ppermute | solution.py:576
  288.1 29.2 %copy-start.2 = (f32[192,128]{1,0:T(8,128)S(1)}, f32[192,128]{1,0:T(8,128)}, u32[]{:S(2)}) copy-start(f32[192,128]{1,0:T(8,128)} %param.22) | copy-start | bytes 294916
  288.1 29.2 %copy-start.4 = (f32[192,128]{1,0:T(8,128)S(1)}, f32[192,128]{1,0:T(8,128)}, u32[]{:S(2)}) copy-start(f32[192,128]{1,0:T(8,128)} %param.23) | copy-start | bytes 294916
  288.1 29.2 %copy-start.5 = (f32[192,128]{1,0:T(8,128)S(1)}, f32[192,128]{1,0:T(8,128)}, u32[]{:S(2)}) copy-start(f32[192,128]{1,0:T(8,128)} %param.24) | copy-start | bytes 294916
  288.1 29.9 %copy-start.3 = (f32[128,192]{0,1:T(8,128)S(1)}, f32[128,192]{0,1:T(8,128)}, u32[]{:S(2)}) copy-start(f32[128,192]{0,1:T(8,128)} %param.19) | copy-start | bytes 294916
  288.1 29.9 %copy-start.6 = (f32[128,192]{0,1:T(8,128)S(1)}, f32[128,192]{0,1:T(8,128)}, u32[]{:S(2)}) copy-start(f32[128,192]{0,1:T(8,128)} %param.20) | copy-start | bytes 294916
  288.1 29.9 %copy-start.7 = (f32[128,192]{0,1:T(8,128)S(1)}, f32[128,192]{0,1:T(8,128)}, u32[]{:S(2)}) copy-start(f32[128,192]{0,1:T(8,128)} %param.21) | copy-start | bytes 294916
  289.9 11.2 %collective-permute-start.8 = (bf16[2,1,192,4,128]{4,2,3,0,1:T(8,128)(2,1)S(1)}, bf16[2,1,192,4,128]{4,2,3,0,1:T(8,128)(2,1)S(1)}, u32[]{:S(2)}, u32[]{:S(2)}) collective-permute-start(bf16[2,1,192,4,128]{4,2,3,0,1:T(8,128)(2,1)S(1)} %dynamic-slice_bitcast_fusion), channel_id=1, source_target_pairs={{0,4},{1,5},{2,6},{3,7},{4,0},{5,1},{6,2},{7,3},{8,12},{9,13},{10,... | collective-permute-start | bytes 1179656 | tf_op jit(solution)/shard_map/ppermute | solution.py:576
  301.2 11.2 %collective-permute-start.9 = (bf16[2,192,2,128]{3,1,2,0:T(8,128)(2,1)S(1)}, bf16[2,192,2,128]{3,1,2,0:T(8,128)(2,1)S(1)}, u32[]{:S(2)}, u32[]{:S(2)}) collective-permute-start(bf16[2,192,2,128]{3,1,2,0:T(8,128)(2,1)S(1)} %dynamic-slice_bitcast_fusion.1), channel_id=1, source_target_pairs={{0,16},{8,24},{16,0},{24,8},{1,17},{9,25},{17,1},{25,9},{2,18},{10... | collective-permute-start | bytes 589832 | tf_op jit(solution)/shard_map/ppermute | solution.py:576
  312.5 4.7 collective-permute-start.10
  318.8 1.7 copy-start.1
